TPU v7x, 128 devices: a whole 4x4x4 slice. The times are simulated.
128 devices in a mesh: ctx: 64 (over y, x, z), head: 2 (over core).
Axes of the slice: x: 4, y: 4, z: 4, core: 2. Of those that a mesh axis runs over, the one named last changes fastest.
Arguments:
- queries: float32 [16384, 2048], P('ctx', 'head')
- keys: float32 [16384, 512], P(('ctx', 'head'))
- values: float32 [16384, 512], P(('ctx', 'head')), may hold values from -6 to 6
- cotangent: float32 [16384, 2048], P('ctx', 'head'), may hold values from -6 to 6
- selected: int32 [16, 3], replicated, may hold values from -1 to 15, as said below
Outputs:
- attended: float32 [16384, 2048], P('ctx', 'head')
- grad_queries: float32 [16384, 2048], P('ctx', 'head')
- grad_keys: float32 [16384, 512], P(('ctx', 'head'))
- grad_values: float32 [16384, 512], P(('ctx', 'head'))
Inputs may be any that keep to these rules, and one draw needn't show every extreme that they name: selected[b, 0] = b; entries 1 and 2 of row b are different blocks before b, except that an entry is -1 when no further block before b is left: row 0 is [0, -1, -1] and row 1 is [1, 0, -1].
All inputs are finite; a program needn't handle non-finite values.
Results may differ from a plain program's by a relative error of at most 0.0003.
Values sent between devices are 32-bit elements; how exact they have to be, the bound alone decides.
No kernel may reach another device: no remote copies, remote signals or barrier semaphores. Data moves between devices by JAX's collectives and lax.ppermute only.
A program may use at most 192 MiB of HBM per device.

v0:
```python
import math
import jax
import jax.numpy as jnp
from jax import lax
from jax.sharding import PartitionSpec as P

QUERY_HEADS = 16
KEY_VALUE_HEADS = 4
HEAD_WIDTH = 128
BLOCK_TOKENS = 1024
TOPK = 3


def block_masks(selected, block_index, query_pos):
    masks = []
    for slot_index in range(TOPK):
        chosen = selected[block_index, slot_index]
        if slot_index == 0:
            key_pos = block_index * BLOCK_TOKENS + jnp.arange(BLOCK_TOKENS, dtype=jnp.int32)
            masks.append(key_pos[None, :] <= query_pos[:, None])
        else:
            masks.append(jnp.broadcast_to(chosen >= 0, (query_pos.shape[0], BLOCK_TOKENS)))
    return jnp.concatenate(masks, 1)


def pick_blocks(whole_keys, whole_values, selected, block_index, kv_heads):
    key_parts, value_parts, offsets = ([], [], [])
    for slot_index in range(TOPK):
        chosen = selected[block_index, slot_index]
        offset = jnp.maximum(chosen, 0) * BLOCK_TOKENS
        offsets.append(offset)
        key_parts.append(lax.dynamic_slice_in_dim(whole_keys, offset, BLOCK_TOKENS, 0))
        value_parts.append(lax.dynamic_slice_in_dim(whole_values, offset, BLOCK_TOKENS, 0))
    picked_keys = jnp.concatenate(key_parts, 0).reshape(TOPK * BLOCK_TOKENS, kv_heads, HEAD_WIDTH)
    picked_values = jnp.concatenate(value_parts, 0).reshape(
        TOPK * BLOCK_TOKENS, kv_heads, HEAD_WIDTH
    )
    return (picked_keys, picked_values, offsets)


def shards(queries, keys, values, cotangent, selected):
    highest = lax.Precision.HIGHEST
    scaling = 1.0 / math.sqrt(HEAD_WIDTH)
    group_width = QUERY_HEADS // KEY_VALUE_HEADS
    local_keys, local_values = (
        lax.all_to_all(keys, "head", split_axis=1, concat_axis=0, tiled=True),
        lax.all_to_all(values, "head", split_axis=1, concat_axis=0, tiled=True),
    )
    tokens_here = local_keys.shape[0]
    width = local_keys.shape[1]
    kv_heads = width // HEAD_WIDTH
    first_position = lax.axis_index("ctx") * tokens_here
    block_index = first_position // BLOCK_TOKENS
    query_pos = first_position + jnp.arange(tokens_here, dtype=jnp.int32)
    allowed = block_masks(selected, block_index, query_pos)
    whole_keys, whole_values = (
        lax.all_gather(local_keys, "ctx", axis=0, tiled=True),
        lax.all_gather(local_values, "ctx", axis=0, tiled=True),
    )
    picked_keys, picked_values, offsets = pick_blocks(
        whole_keys, whole_values, selected, block_index, kv_heads
    )
    block_of_queries = queries.reshape(tokens_here, kv_heads, group_width, HEAD_WIDTH)
    cotangent_block = cotangent.reshape(tokens_here, kv_heads, group_width, HEAD_WIDTH)
    scores = scaling * jnp.einsum(
        "thgd,shd->hgts", block_of_queries, picked_keys, precision=highest
    )
    scores = jnp.where(allowed[None, None], scores, -jnp.inf)
    maximum = jnp.max(scores, axis=-1, keepdims=True)
    probs = jnp.exp(scores - maximum)
    probs = probs / jnp.sum(probs, axis=-1, keepdims=True)
    attended = jnp.einsum("hgts,shd->thgd", probs, picked_values, precision=highest)
    row_dots = jnp.transpose(jnp.sum(cotangent_block * attended, axis=-1), (1, 2, 0))
    grad_probs = jnp.einsum("thgd,shd->hgts", cotangent_block, picked_values, precision=highest)
    grad_scores = probs * (grad_probs - row_dots[..., None])
    query_gradient = scaling * jnp.einsum(
        "hgts,shd->thgd", grad_scores, picked_keys, precision=highest
    )
    grad_k_sel = scaling * jnp.einsum(
        "hgts,thgd->shd", grad_scores, block_of_queries, precision=highest
    )
    grad_v_sel = jnp.einsum("hgts,thgd->shd", probs, cotangent_block, precision=highest)
    seq_rows = whole_keys.shape[0]
    key_gradient_total = jnp.zeros((seq_rows, kv_heads, HEAD_WIDTH), jnp.float32)
    value_gradient_total = jnp.zeros((seq_rows, kv_heads, HEAD_WIDTH), jnp.float32)
    for slot_index in range(TOPK):
        offset = offsets[slot_index]
        piece_k = grad_k_sel[slot_index * BLOCK_TOKENS : (slot_index + 1) * BLOCK_TOKENS]
        piece_v = grad_v_sel[slot_index * BLOCK_TOKENS : (slot_index + 1) * BLOCK_TOKENS]
        key_gradient_total = lax.dynamic_update_slice_in_dim(
            key_gradient_total,
            lax.dynamic_slice_in_dim(key_gradient_total, offset, BLOCK_TOKENS, 0) + piece_k,
            offset,
            0,
        )
        value_gradient_total = lax.dynamic_update_slice_in_dim(
            value_gradient_total,
            lax.dynamic_slice_in_dim(value_gradient_total, offset, BLOCK_TOKENS, 0) + piece_v,
            offset,
            0,
        )
    owned_k, owned_v = (
        lax.psum_scatter(
            key_gradient_total.reshape(seq_rows, width), "ctx", scatter_dimension=0, tiled=True
        ),
        lax.psum_scatter(
            value_gradient_total.reshape(seq_rows, width), "ctx", scatter_dimension=0, tiled=True
        ),
    )
    grad_keys, grad_values = (
        lax.all_to_all(owned_k, "head", split_axis=0, concat_axis=1, tiled=True),
        lax.all_to_all(owned_v, "head", split_axis=0, concat_axis=1, tiled=True),
    )
    return (
        attended.reshape(tokens_here, -1),
        query_gradient.reshape(tokens_here, -1),
        grad_keys,
        grad_values,
    )


def solution(mesh):
    placed = (
        P("ctx", "head"),
        P(("ctx", "head"), None),
        P(("ctx", "head"), None),
        P("ctx", "head"),
        P(),
    )
    return jax.shard_map(
        shards,
        mesh=mesh,
        in_specs=placed,
        out_specs=(
            P("ctx", "head"),
            P("ctx", "head"),
            P(("ctx", "head"), None),
            P(("ctx", "head"), None),
        ),
        check_vma=False,
    )
```

profile of v0, /device:TPU:1, one launch (start us, length us, event | category | flops | bytes accessed | tf_op | source)
XLA Modules:
  0.0 1183.8 jit_solution(17859586762684518673)
XLA Ops:
  7.2 1.1 copy.79
  8.3 5.0 all_to_all.76
  13.3 0.8 copy.80
  14.2 0.0 all-gather.3.cloned.1.call-start
  14.2 1.1 copy.76
  15.3 0.1 copy.77
  15.4 3.9 all_to_all.77
  19.4 0.8 copy.78
  20.2 0.0 reduce-scatter.3.cloned.1.call-start
  20.3 1.4 constant_dynamic-slice_fusion.6
  24.8 2.5 copy.85
  27.3 2.6 copy.115
  29.9 0.2 broadcast_compare_fusion
  30.1 3.9 add_add_fusion
  34.1 86.8 %all-gather.5.cloned.1.call-done = f32[16384,256]{1,0:T(8,128)} async-done(((f32[256,256]{1,0:T(8,128)}), f32[16384,256]{1,0:T(8,128)}) %all-gather.5.cloned.1.call-update) | async-done | bytes 16777232 | tf_op jit(solution)/shard_map/all_gather | solution.py:57
  120.9 2.2 constant_dynamic-slice_fusion.2
  123.1 1.8 pad_maximum_fusion.1
  124.9 2.4 copy.81
  127.3 24.6 %fusion.3 = (f32[2,4,256]{2,1,0:T(4,128)S(1)}, f32[2,3072,256,4]{2,1,3,0:T(8,128)S(1)}) fusion(pred[256,3072]{0,1:T(8,128)(4,1)} %add_add_fusion, f32[3072,2,128,1]{0,2,3,1:T(8,128)S(1)} %bitcast.93, f32[256,2,4,128]{0,3,2,1:T(8,128)} %bitcast.95), kind=kOutput, calls=%fused_computation.6 | convolution fusion | flops 9682548736 | bytes 30154752 | tf_op jit(solution)/shard_map/thgd,shd->hgts/dot_general | solution.py:65
  151.9 8.6 copy-done
  160.6 5.3 fusion.2
  165.8 77.2 %all-gather.3.cloned.1.call-done = f32[16384,256]{0,1:T(8,128)} async-done(((f32[256,256]{0,1:T(8,128)}), f32[16384,256]{0,1:T(8,128)}) %all-gather.3.cloned.1.call-update) | async-done | bytes 16777232 | tf_op jit(solution)/shard_map/all_gather | solution.py:58
  243.1 2.3 constant_dynamic-slice_fusion.5
  245.3 2.0 pad_maximum_fusion
  247.3 25.6 %fusion.10 = (f32[256,2,4]{0,2,1:T(4,128)S(1)}, f32[2,128,4,256]{3,1,2,0:T(8,128)}) fusion(f32[256,1024]{0,1:T(8,128)S(1)} %copy-done.7, f32[3072,2,128,1]{0,2,3,1:T(8,128)} %bitcast.98, f32[2,3072,256,4]{2,1,3,0:T(8,128)} %copy-done, f32[2,4,256]{2,1,0:T(4,128)S(1)} %fusion.2, f32[2,4,256]{2,1,0:T(4,128)S(1)} %get-tuple-element.33, ...), kind=kOutput, calls=%fused_computation.26 | convolution fusion | flops 9689364480 | bytes 31219712 | tf_op jit(solution)/shard_map/hgts,shd->thgd/dot_general | solution.py:72
  272.9 34.7 %convolution_bitcast_fusion = f32[3072,2,128]{0,2,1:T(8,128)S(1)} fusion(f32[256,2,4,128]{0,3,2,1:T(8,128)S(1)} %bitcast.100, f32[2,3072,256,4]{2,1,3,0:T(8,128)} %copy-done, f32[2,4,256]{2,1,0:T(4,128)S(1)} %fusion.2, f32[2,4,256]{2,1,0:T(4,128)S(1)} %get-tuple-element.33, pred[256,3072]{0,1:T(8,128)(4,1)S(1)} %copy-done.5), kind=kOutput, calls=%fused_computation.7 | convolution fusion | flops 9688842240 | bytes 30162944 | tf_op jit(solution)/shard_map/hgts,thgd->shd/dot_general | solution.py:82
  307.7 34.6 %fusion = f32[2,4,256,3072]{2,3,1,0:T(8,128)} fusion(f32[2,4,256]{2,1,0:T(4,128)S(1)} %bitcast.112, f32[3072,2,128,1]{0,2,3,1:T(8,128)} %bitcast.99, f32[256,2,4,128]{0,3,2,1:T(8,128)S(1)} %bitcast.101, f32[2,4,256]{2,1,0:T(4,128)S(1)} %fusion.2, f32[2,4,256]{2,1,0:T(4,128)S(1)} %get-tuple-element.33, f32[2,3072,256,4]{2,1,3,0:T(8,128)} %copy-done, ...), kind=kOutput, calls=%fused_computation.1 | convolution fusion | flops 9701425152 | bytes 55336960 | tf_op jit(solution)/shard_map/thgd,shd->hgts/dot_general | solution.py:74
  342.2 29.3 %fusion.5 = f32[3072,2,128]{0,2,1:T(8,128)S(1)} fusion(f32[2,4,256,3072]{2,3,1,0:T(8,128)} %fusion, f32[256,2,4,128]{0,3,2,1:T(8,128)S(1)} %bitcast.96), kind=kOutput, calls=%fused_computation.10 | convolution fusion | flops 9664462848 | bytes 29360128 | tf_op jit(solution)/shard_map/hgts,thgd->shd/dot_general | solution.py:79
  371.5 7.7 broadcast.22.clone
  379.2 1.1 slice_dynamic-update-slice_fusion
  380.2 7.7 broadcast.22.clone.1
  387.9 1.1 slice_dynamic-update-slice_fusion.1
  389.0 3.4 fusion.7
  392.4 2.3 fusion.8
  394.8 2.8 fusion.6
  397.7 2.5 copy.96
  400.2 18.0 %convolution_multiply_fusion = f32[2,128,4,256]{3,1,2,0:T(8,128)} fusion(f32[3072,2,128,1]{0,2,3,1:T(8,128)S(1)} %bitcast.94, f32[2,4,256,3072]{2,3,1,0:T(8,128)} %fusion), kind=kOutput, calls=%fused_computation.14 | convolution fusion | flops 9663938560 | bytes 29360128 | tf_op jit(solution)/shard_map/hgts,shd->thgd/dot_general | solution.py:76
  418.2 2.5 copy.97
  420.7 313.6 %reduce-scatter.3.cloned.1.call-done = f32[256,256]{0,1:T(8,128)} async-done(((f32[16384,256]{0,1:T(8,128)}), f32[256,256]{0,1:T(8,128)}) %reduce-scatter.3.cloned.1.call-update) | async-done | bytes 262160 | tf_op jit(solution)/shard_map/reduce_scatter | solution.py:103
  734.3 1.1 copy.91
  735.4 54.5 %all_to_all.78 = f32[2,128,256]{2,1,0:T(8,128)S(1)} all-to-all(f32[2,128,256]{2,1,0:T(8,128)S(1)} %bitcast.106), channel_id=1, replica_groups=mesh['ctx'=64,'head'=2] {'head'}, dimensions={0} | all-to-all | bytes 524288 | tf_op jit(solution)/shard_map/all_to_all | solution.py:111
  789.9 0.1 copy.92
  790.0 0.8 copy.98
  790.9 329.5 %reduce-scatter.5.cloned.1.call-done = f32[256,256]{0,1:T(8,128)} async-done(((f32[16384,256]{0,1:T(8,128)}), f32[256,256]{0,1:T(8,128)}) %reduce-scatter.5.cloned.1.call-update) | async-done | bytes 262160 | tf_op jit(solution)/shard_map/reduce_scatter | solution.py:106
  1120.4 1.1 copy.94
  1121.5 54.6 %all_to_all.79 = f32[2,128,256]{2,1,0:T(8,128)S(1)} all-to-all(f32[2,128,256]{2,1,0:T(8,128)S(1)} %bitcast.108), channel_id=1, replica_groups=mesh['ctx'=64,'head'=2] {'head'}, dimensions={0} | all-to-all | bytes 524288 | tf_op jit(solution)/shard_map/all_to_all | solution.py:112
  1176.1 0.1 copy.95
  1176.2 0.8 copy.99
  (27 shorter events, 0.2 us)
Async XLA Ops:
  7.2 113.7 %all-gather.5.cloned.1.call-start = ((), (), s32[]{:S(2)}) async-start(), calls=%async_computation.7 | async-start | bytes 17039360 | tf_op jit(solution)/shard_map/all_gather | solution.py:57
  14.2 228.9 %all-gather.3.cloned.1.call-start = ((), (), s32[]{:S(2)}) async-start(), calls=%async_computation.6 | async-start | bytes 17039360 | tf_op jit(solution)/shard_map/all_gather | solution.py:58
  20.2 714.1 %reduce-scatter.3.cloned.1.call-start = ((), (), s32[]{:S(2)}) async-start(), calls=%async_computation.8 | async-start | bytes 17039360 | tf_op jit(solution)/shard_map/reduce_scatter | solution.py:103
  127.3 24.6 %copy-start.1 = (f32[3072,256]{0,1:T(8,128)}, f32[3072,256]{0,1:T(8,128)S(1)}, u32[]{:S(2)}) copy-start(f32[3072,256]{0,1:T(8,128)S(1)} %copy.81) | copy-start | bytes 9437188
  127.3 33.3 %copy-start.4 = (pred[256,3072]{0,1:T(8,128)(4,1)S(1)}, pred[256,3072]{0,1:T(8,128)(4,1)}, u32[]{:S(2)}) copy-start(pred[256,3072]{0,1:T(8,128)(4,1)} %add_add_fusion) | copy-start | bytes 2359300
  151.9 8.7 copy-start
  160.6 86.7 %copy-start.5 = (pred[256,3072]{0,1:T(8,128)(4,1)S(1)}, pred[256,3072]{0,1:T(8,128)(4,1)}, u32[]{:S(2)}) copy-start(pred[256,3072]{0,1:T(8,128)(4,1)} %add_add_fusion) | copy-start | bytes 2359300
  160.6 86.7 %copy-start.7 = (f32[256,1024]{0,1:T(8,128)S(1)}, f32[256,1024]{0,1:T(8,128)}, u32[]{:S(2)}) copy-start(f32[256,1024]{0,1:T(8,128)} %copy.85) | copy-start | bytes 3145732
  307.6 81.3 %copy-start.6 = (f32[3072,2,128]{0,2,1:T(8,128)}, f32[3072,2,128]{0,2,1:T(8,128)S(1)}, u32[]{:S(2)}) copy-start(f32[3072,2,128]{0,2,1:T(8,128)S(1)} %convolution_bitcast_fusion) | copy-start | bytes 9437188
  307.7 34.6 %copy-start.3 = (f32[256,1024]{0,1:T(8,128)S(1)}, f32[256,1024]{0,1:T(8,128)}, u32[]{:S(2)}) copy-start(f32[256,1024]{0,1:T(8,128)} %copy.115) | copy-start | bytes 3145732
  394.7 5.5 copy-start.2
  394.7 725.6 %reduce-scatter.5.cloned.1.call-start = ((), (), s32[]{:S(2)}) async-start(), calls=%async_computation.9 | async-start | bytes 17039360 | tf_op jit(solution)/shard_map/reduce_scatter | solution.py:106
Sparse Core Ops, SparseCore 0:
  14.3 106.5 all-gather.4
  124.1 118.8 all-gather.2
  394.9 339.4 reduce-scatter.2
  736.6 383.7 reduce-scatter.4
where the time goes:
time: 1190 us; the launch traced here: 1180 us
  waiting for transfers between devices  807 us (68%)
  matrix products  167 us (14%)
  blocking collectives  118 us (10%)
  local copies, waits for them, and re-layouts  52.6 us (4%)
  other arithmetic  21.8 us (2%)
  between operations  17.2 us (1%)
    reduce_scatter x1, waiting for transfers between devices, shards(): lax.psum_scatter(value_gradient_total.reshape(seq_rows, width), 'ctx', sc...  330 us
    reduce_scatter x1, waiting for transfers between devices, shards(): lax.psum_scatter(key_gradient_total.reshape(seq_rows, width), 'ctx', scat...  314 us
    all_gather x1, waiting for transfers between devices, shards(): lax.all_gather(local_keys, 'ctx', axis=0, tiled=True)  86.8 us
    all_gather x1, waiting for transfers between devices, shards(): lax.all_gather(local_values, 'ctx', axis=0, tiled=True)  77.2 us
    all_to_all x1, blocking collectives, shards(): lax.all_to_all(owned_v, 'head', split_axis=0, concat_axis=1, tiled=True)  54.6 us
    all_to_all x1, blocking collectives, shards(): lax.all_to_all(owned_k, 'head', split_axis=0, concat_axis=1, tiled=True)  54.5 us
    dot_general x1, matrix products, shards(): jnp.einsum('hgts,thgd->shd', probs, cotangent_block, precision=highest)  34.7 us
    dot_general x1, matrix products, shards(): jnp.einsum('thgd,shd->hgts', cotangent_block, picked_values, precision=hi...  34.6 us
  transfers between devices with their start and end apart: 4, of which 4 were waited for; matrix products, arithmetic and copies ran while one was open for 6% of the time, Pallas kernels for 0%

commit v1 on v0

--- a/solution.py
+++ b/solution.py
@@ -54,7 +54,9 @@
     query_pos = first_position + jnp.arange(tokens_here, dtype=jnp.int32)
     allowed = block_masks(selected, block_index, query_pos)
     whole_keys, whole_values = (
-        lax.all_gather(local_keys, "ctx", axis=0, tiled=True),
+        jnp.concatenate(
+            lax.all_to_all(jnp.stack([local_keys] * lax.axis_size("ctx")), "ctx", 0, 0), axis=0
+        ),
         lax.all_gather(local_values, "ctx", axis=0, tiled=True),
     )
     picked_keys, picked_values, offsets = pick_blocks(

time: 1190 us -> 1260 us (1.059)
  waiting for transfers between devices: 807 us -> 861 us
  local copies, waits for them, and re-layouts: 52.6 us -> 65.3 us
    all_to_all x0 -> x1, waiting for transfers between devices: none -> 281 us  [shards(): lax.all_to_all(jnp.stack([local_keys] * lax.axis_size('ctx')), 'ctx', 0, 0)]
    reduce_scatter x1, waiting for transfers between devices: 330 us -> 226 us  [shards(): lax.psum_scatter(value_gradient_total.reshape(seq_rows, width), 'ctx', sc...]
    all_gather x1 -> x0, waiting for transfers between devices: 86.8 us -> none  [shards(): lax.all_gather(local_keys, 'ctx', axis=0, tiled=True)]
    all_gather x1, waiting for transfers between devices: 77.2 us -> 21.9 us  [shards(): lax.all_gather(local_values, 'ctx', axis=0, tiled=True)]
    reduce_scatter x1, waiting for transfers between devices: 314 us -> 333 us  [shards(): lax.psum_scatter(key_gradient_total.reshape(seq_rows, width), 'ctx', scat...]
  transfers between devices with their start and end apart: 4 -> 4, of which waited for: 4 -> 4; matrix products, arithmetic and copies ran while one was open for 6% -> 13% of each run, Pallas kernels for 0% -> 0%
where the time goes in v1:
time: 1260 us; the launch traced here: 1250 us
  waiting for transfers between devices  861 us (68%)
  matrix products  164 us (13%)
  blocking collectives  112 us (9%)
  local copies, waits for them, and re-layouts  65.3 us (5%)
  other arithmetic  22.8 us (2%)
  between operations  17.7 us (1%)
    reduce_scatter x1, waiting for transfers between devices, shards(): lax.psum_scatter(key_gradient_total.reshape(seq_rows, width), 'ctx', scat...  333 us
    all_to_all x1, waiting for transfers between devices, shards(): lax.all_to_all(jnp.stack([local_keys] * lax.axis_size('ctx')), 'ctx', 0, 0)  281 us
    reduce_scatter x1, waiting for transfers between devices, shards(): lax.psum_scatter(value_gradient_total.reshape(seq_rows, width), 'ctx', sc...  226 us
    all_to_all x1, blocking collectives, shards(): lax.all_to_all(owned_k, 'head', split_axis=0, concat_axis=1, tiled=True)  52.9 us
    all_to_all x1, blocking collectives, shards(): lax.all_to_all(owned_v, 'head', split_axis=0, concat_axis=1, tiled=True)  50.3 us
    dot_general x1, matrix products, shards(): jnp.einsum('hgts,thgd->shd', probs, cotangent_block, precision=highest)  34.9 us
    dot_general x1, matrix products, shards(): jnp.einsum('thgd,shd->hgts', cotangent_block, picked_values, precision=hi...  33.5 us
    dot_general x1, matrix products, shards(): jnp.einsum('hgts,thgd->shd', grad_scores, block_of_queries, precision=hig...  29.4 us
  transfers between devices with their start and end apart: 4, of which 4 were waited for; matrix products, arithmetic and copies ran while one was open for 13% of the time, Pallas kernels for 0%

profile of v1, /device:TPU:1, one launch (start us, length us, event | category | flops | bytes accessed | tf_op | source)
XLA Modules:
  0.0 1254.5 jit_solution(1029927319020621291)
XLA Ops:
  7.2 1.1 copy.77
  8.3 0.1 copy.78
  8.4 5.0 all_to_all.78
  13.4 0.8 copy.79
  14.3 1.1 copy.80
  15.4 3.9 all_to_all.79
  19.3 0.1 copy.81
  19.5 0.1 copy.82
  19.6 7.8 stack.5
  27.4 11.7 all-to-all-start.2
  39.2 0.6 constant_dynamic-slice_fusion.6
  43.1 0.3 copy.117
  43.4 1.3 copy.87
  44.7 0.2 broadcast_compare_fusion
  44.9 3.9 add_add_fusion
  48.9 280.5 %all-to-all-done.2 = f32[64,256,256]{1,2,0:T(8,128)} async-done(((f32[64,256,256]{1,2,0:T(8,128)}), f32[64,256,256]{1,2,0:T(8,128)}, u32[]{:S(2)}, u32[]{:S(2)}) %all-to-all-start.2) | async-done | bytes 16777248 | tf_op jit(solution)/shard_map/all_to_all | solution.py:58
  329.4 11.7 copy.118
  341.1 21.9 %all-gather.2.cloned.1.call-done = f32[16384,256]{0,1:T(8,128)} async-done(((f32[256,256]{0,1:T(8,128)}), f32[16384,256]{0,1:T(8,128)}) %all-gather.2.cloned.1.call-update) | async-done | bytes 16777232 | tf_op jit(solution)/shard_map/all_gather | solution.py:60
  362.9 4.8 constant_dynamic-slice_fusion.2
  367.7 0.3 pad_maximum_fusion.1
  368.1 22.8 %fusion.3 = (f32[2,4,256]{2,1,0:T(4,128)S(1)}, f32[2,3072,256,4]{2,1,3,0:T(8,128)S(1)}) fusion(pred[256,3072]{0,1:T(8,128)(4,1)S(1)} %copy-done.3, f32[3072,2,128,1]{0,2,3,1:T(8,128)S(1)} %bitcast.96, f32[256,2,4,128]{0,3,2,1:T(8,128)S(1)} %bitcast.98), kind=kOutput, calls=%fused_computation.6 | convolution fusion | flops 9682548736 | bytes 30154752 | tf_op jit(solution)/shard_map/thgd,shd->hgts/dot_general | solution.py:67
  390.9 8.7 copy-done
  399.6 5.4 fusion.2
  405.0 34.9 %convolution_bitcast_fusion = f32[3072,2,128]{0,2,1:T(8,128)S(1)} fusion(f32[256,2,4,128]{0,3,2,1:T(8,128)S(1)} %bitcast.103, f32[2,3072,256,4]{2,1,3,0:T(8,128)} %copy-done, f32[2,4,256]{2,1,0:T(4,128)S(1)} %fusion.2, f32[2,4,256]{2,1,0:T(4,128)S(1)} %get-tuple-element.33, pred[256,3072]{0,1:T(8,128)(4,1)S(1)} %copy-done.3), kind=kOutput, calls=%fused_computation.7 | convolution fusion | flops 9688842240 | bytes 30162944 | tf_op jit(solution)/shard_map/hgts,thgd->shd/dot_general | solution.py:84
  440.0 7.7 broadcast.23.clone.1
  447.6 1.1 slice_dynamic-update-slice_fusion
  448.7 2.4 fusion.7
  451.1 2.4 fusion.6
  453.5 3.2 pad_maximum_fusion
  456.7 25.3 %fusion.10 = (f32[256,2,4]{0,2,1:T(4,128)S(1)}, f32[2,128,4,256]{3,1,2,0:T(8,128)}) fusion(f32[256,1024]{0,1:T(8,128)} %copy.87, f32[3072,2,128,1]{0,2,3,1:T(8,128)} %bitcast.101, f32[2,3072,256,4]{2,1,3,0:T(8,128)} %copy-done, f32[2,4,256]{2,1,0:T(4,128)S(1)} %fusion.2, f32[2,4,256]{2,1,0:T(4,128)S(1)} %get-tuple-element.33, pred[256,3072]{0,1:T(8,128)(4,1)} %add_add_fusion), kind=kOutput, calls=%fused_computation.26 | convolution fusion | flops 9689364480 | bytes 31219712 | tf_op jit(solution)/shard_map/hgts,shd->thgd/dot_general | solution.py:74
  482.0 33.5 %fusion = f32[2,4,256,3072]{2,3,1,0:T(8,128)} fusion(f32[2,4,256]{2,1,0:T(4,128)S(1)} %bitcast.115, f32[3072,2,128,1]{0,2,3,1:T(8,128)} %bitcast.102, f32[256,2,4,128]{0,3,2,1:T(8,128)S(1)} %bitcast.104, f32[2,4,256]{2,1,0:T(4,128)S(1)} %fusion.2, f32[2,4,256]{2,1,0:T(4,128)S(1)} %get-tuple-element.33, f32[2,3072,256,4]{2,1,3,0:T(8,128)} %copy-done, ...), kind=kOutput, calls=%fused_computation.1 | convolution fusion | flops 9701425152 | bytes 55336960 | tf_op jit(solution)/shard_map/thgd,shd->hgts/dot_general | solution.py:76
  515.6 29.4 %fusion.5 = f32[3072,2,128]{0,2,1:T(8,128)S(1)} fusion(f32[2,4,256,3072]{2,3,1,0:T(8,128)} %fusion, f32[256,2,4,128]{0,3,2,1:T(8,128)S(1)} %bitcast.99), kind=kOutput, calls=%fused_computation.10 | convolution fusion | flops 9664462848 | bytes 29360128 | tf_op jit(solution)/shard_map/hgts,thgd->shd/dot_general | solution.py:81
  545.0 7.7 broadcast.23.clone
  552.7 1.1 slice_dynamic-update-slice_fusion.1
  553.8 2.6 fusion.9
  556.4 2.4 fusion.8
  558.9 18.1 %convolution_multiply_fusion = f32[2,128,4,256]{3,1,2,0:T(8,128)} fusion(f32[3072,2,128,1]{0,2,3,1:T(8,128)S(1)} %bitcast.97, f32[2,4,256,3072]{2,3,1,0:T(8,128)} %fusion), kind=kOutput, calls=%fused_computation.14 | convolution fusion | flops 9663938560 | bytes 29360128 | tf_op jit(solution)/shard_map/hgts,shd->thgd/dot_general | solution.py:78
  576.9 2.5 copy.99
  579.5 2.5 copy.98
  582.0 225.7 %reduce-scatter.5.cloned.1.call-done = f32[256,256]{0,1:T(8,128)} async-done(((f32[16384,256]{0,1:T(8,128)}), f32[256,256]{0,1:T(8,128)}) %reduce-scatter.5.cloned.1.call-update) | async-done | bytes 262160 | tf_op jit(solution)/shard_map/reduce_scatter | solution.py:108
  807.8 1.1 copy.96
  808.8 50.3 %all_to_all.80 = f32[2,128,256]{2,1,0:T(8,128)S(1)} all-to-all(f32[2,128,256]{2,1,0:T(8,128)S(1)} %bitcast.109), channel_id=1, replica_groups=mesh['ctx'=64,'head'=2] {'head'}, dimensions={0} | all-to-all | bytes 524288 | tf_op jit(solution)/shard_map/all_to_all | solution.py:114
  859.1 0.1 copy.97
  859.2 0.8 copy.101
  860.1 332.5 %reduce-scatter.3.cloned.1.call-done = f32[256,256]{0,1:T(8,128)} async-done(((f32[16384,256]{0,1:T(8,128)}), f32[256,256]{0,1:T(8,128)}) %reduce-scatter.3.cloned.1.call-update) | async-done | bytes 262160 | tf_op jit(solution)/shard_map/reduce_scatter | solution.py:105
  1192.6 1.1 copy.93
  1193.7 52.9 %all_to_all.81 = f32[2,128,256]{2,1,0:T(8,128)S(1)} all-to-all(f32[2,128,256]{2,1,0:T(8,128)S(1)} %bitcast.111), channel_id=1, replica_groups=mesh['ctx'=64,'head'=2] {'head'}, dimensions={0} | all-to-all | bytes 524288 | tf_op jit(solution)/shard_map/all_to_all | solution.py:113
  1246.7 0.8 copy.100
  (32 shorter events, 0.4 us)
Async XLA Ops:
  7.2 355.8 %all-gather.2.cloned.1.call-start = ((), (), s32[]{:S(2)}) async-start(), calls=%async_computation.7 | async-start | bytes 17039360 | tf_op jit(solution)/shard_map/all_gather | solution.py:60
  27.4 11.8 copy-start.9
  27.4 15.7 %copy-start.5 = (f32[256,1024]{1,0:T(8,128)S(1)}, f32[256,1024]{1,0:T(8,128)}, u32[]{:S(2)}) copy-start(f32[256,1024]{1,0:T(8,128)} %param.5) | copy-start | bytes 3145732
  27.4 16.0 %copy-start.6 = (f32[256,1024]{1,0:T(8,128)S(1)}, f32[256,1024]{1,0:T(8,128)}, u32[]{:S(2)}) copy-start(f32[256,1024]{1,0:T(8,128)} %param.8) | copy-start | bytes 3145732
  27.4 302.0 %all-to-all-start.2 = ((f32[64,256,256]{1,2,0:T(8,128)}), f32[64,256,256]{1,2,0:T(8,128)}, u32[]{:S(2)}, u32[]{:S(2)}) async-start(f32[64,256,256]{1,2,0:T(8,128)} %stack.5), calls=%async_computation.2 | async-start | bytes 33554432 | tf_op jit(solution)/shard_map/all_to_all | solution.py:58
  39.1 768.7 %reduce-scatter.5.cloned.1.call-start = ((), (), s32[]{:S(2)}) async-start(), calls=%async_computation.9 | async-start | bytes 17039360 | tf_op jit(solution)/shard_map/reduce_scatter | solution.py:108
  362.9 5.2 copy-start.3
  368.1 22.8 %copy-start.1 = (f32[3072,256]{0,1:T(8,128)}, f32[3072,256]{0,1:T(8,128)S(1)}, u32[]{:S(2)}) copy-start(f32[3072,256]{0,1:T(8,128)S(1)} %pad_maximum_fusion.1) | copy-start | bytes 9437188
  390.9 8.7 copy-start
  390.9 14.1 %copy-start.7 = (f32[256,1024]{0,1:T(8,128)S(1)}, f32[256,1024]{0,1:T(8,128)}, u32[]{:S(2)}) copy-start(f32[256,1024]{0,1:T(8,128)} %copy.87) | copy-start | bytes 3145732
  453.5 739.1 %reduce-scatter.3.cloned.1.call-start = ((), (), s32[]{:S(2)}) async-start(), calls=%async_computation.8 | async-start | bytes 17039360 | tf_op jit(solution)/shard_map/reduce_scatter | solution.py:105
  456.7 25.3 %copy-start.4 = (pred[256,3072]{0,1:T(8,128)(4,1)S(1)}, pred[256,3072]{0,1:T(8,128)(4,1)}, u32[]{:S(2)}) copy-start(pred[256,3072]{0,1:T(8,128)(4,1)} %add_add_fusion) | copy-start | bytes 2359300
  456.7 25.3 %copy-start.8 = (f32[256,1024]{0,1:T(8,128)S(1)}, f32[256,1024]{0,1:T(8,128)}, u32[]{:S(2)}) copy-start(f32[256,1024]{0,1:T(8,128)} %copy.87) | copy-start | bytes 3145732
  552.7 6.2 copy-start.2
Sparse Core Ops, SparseCore 0:
  14.4 348.4 all-gather.1
  453.6 354.1 reduce-scatter.4
  810.2 382.4 reduce-scatter.2
